TPU v7x, 32 devices: a whole 2x2x4 slice. The times are simulated.
32 devices in a mesh: space: 8 (over y, x, core), vec: 4 (over z).
Axes of the slice: x: 2, y: 2, z: 4, core: 2. Of those that a mesh axis runs over, the one named last changes fastest.
Arguments:
- vectors: float32 [2, 3, 384, 8, 2048], P(None, None, 'vec', 'space'), may hold values from -0.375 to 0.375
- links: float32 [3, 2, 3, 3, 8, 2048], P(None, None, None, None, 'space'), may hold values from -3.5 to 3.5
- momenta: int32 [2, 3], replicated, may hold values from -2 to 2
- directions: int32 [3], replicated, may hold values from 0 to 2, each once
Outputs:
- elementals: float32 [2, 3, 2, 384, 384], P(None, None, None, 'space', 'vec')
Inputs may be any that keep to these rules, and one draw needn't show every extreme that they name: directions holds each of 0, 1, 2 once.
All inputs are finite; a program needn't handle non-finite values.
Results may differ from a plain program's by a relative error of at most 0.000098.
Values sent between devices are 32-bit elements; how exact they have to be, the bound alone decides.
No kernel may reach another device: no remote copies, remote signals or barrier semaphores. Data moves between devices by JAX's collectives and lax.ppermute only.
A program may use at most 128 MiB of HBM per device.

v0:
```python
import jax
import jax.numpy as jnp
from jax import lax
from jax.sharding import PartitionSpec as P

LY = 32
LZ = 64


def padded_2(shard, sides, width):
    for axis, dim in sides:
        size, length = (lax.axis_size(axis), shard.shape[dim])
        up = [(i, (i + 1) % size) for i in range(size)]
        down = [(j, i) for i, j in up]
        last = lax.slice_in_dim(shard, length - width, length, axis=dim)
        first = lax.slice_in_dim(shard, 0, width, axis=dim)
        before = lax.ppermute(last, axis, up)
        after = lax.ppermute(first, axis, down)
        shard = jnp.concatenate([before, shard, after], axis=dim)
    return shard


def shifted(value, axis, steps):
    count = lax.axis_size(axis)
    pairs = [(source, (source + steps) % count) for source in range(count)]
    return lax.ppermute(value, axis, pairs)


def site_shift(field, mu, step, plane_y, plane_z):
    shape = field.shape
    cube = field.reshape(shape[:-1] + (plane_y, plane_z))
    cube = jnp.roll(cube, -step, axis=-3 + mu)
    return cube.reshape(shape)


def color_apply(link, field, dagger):
    link_re = link[0]
    link_im = link[1]
    if dagger:
        link_re = jnp.swapaxes(link_re, 0, 1)
        link_im = -jnp.swapaxes(link_im, 0, 1)
    link_re = link_re[:, :, None]
    link_im = link_im[:, :, None]
    field_re = field[0][None]
    field_im = field[1][None]
    out_re = jnp.sum(link_re * field_re - link_im * field_im, axis=1)
    out_im = jnp.sum(link_re * field_im + link_im * field_re, axis=1)
    return jnp.stack([out_re, out_im], 0)


def phase_tables(momenta, xcoord, sites, extent_x, plane_y, plane_z):
    ycoord = sites // plane_z
    zcoord = sites % plane_z
    p0 = momenta[:, 0][:, None, None]
    p1 = momenta[:, 1][:, None, None]
    p2 = momenta[:, 2][:, None, None]
    frac = (p0 * xcoord % extent_x).astype(jnp.float32) / extent_x
    frac = frac + (p1 * ycoord[None, None] % plane_y).astype(jnp.float32) / plane_y
    frac = frac + (p2 * zcoord[None, None] % plane_z).astype(jnp.float32) / plane_z
    theta = 2.0 * jnp.pi * frac
    return (jnp.cos(theta), jnp.sin(theta))


def elemental_block(left_vecs, right_disp, cosine, sine):
    vec_re = left_vecs[0][None]
    vec_im = left_vecs[1][None]
    cosine = cosine[:, None, None]
    sine = sine[:, None, None]
    left_re = vec_re * cosine - vec_im * sine
    left_im = -(vec_re * sine + vec_im * cosine)
    left = jnp.stack([left_re, left_im], 1)
    gram = jnp.einsum(
        "mpcaxs,dqcbxs->mpadqb",
        left,
        right_disp,
        precision=lax.Precision.HIGHEST,
        preferred_element_type=jnp.float32,
    )
    part_re = gram[:, 0, :, :, 0] - gram[:, 1, :, :, 1]
    part_im = gram[:, 0, :, :, 1] + gram[:, 1, :, :, 0]
    stacked = jnp.stack([part_re, part_im], 1)
    return jnp.transpose(stacked, (0, 3, 1, 2, 4))


def on_device(vectors, links, momenta, directions):
    plane_y = LY
    plane_z = LZ
    extent_x = lax.axis_size("space")
    xcoord = lax.axis_index("space")
    padded = padded_2(vectors, (("space", 3),), 1)
    lower = shifted(links[0], "space", 1)
    forward_x = color_apply(links[0], padded[:, :, :, 2:3], False)
    backward_x = color_apply(lower, padded[:, :, :, 0:1], True)
    displaced_list = [forward_x - backward_x]
    for mu in (1, 2):
        forward = color_apply(links[mu], site_shift(vectors, mu, 1, plane_y, plane_z), False)
        backward = site_shift(color_apply(links[mu], vectors, True), mu, -1, plane_y, plane_z)
        displaced_list.append(forward - backward)
    displaced = jnp.stack(displaced_list, 0)
    site_count = vectors.shape[4]
    sites = jnp.arange(site_count, dtype=jnp.int32)
    cosine, sine = phase_tables(momenta, xcoord, sites, extent_x, plane_y, plane_z)
    block = elemental_block(
        lax.all_gather(vectors, "vec", axis=2, tiled=True), displaced, cosine, sine
    )
    reduced = lax.psum_scatter(block, "space", scatter_dimension=3, tiled=True)
    return jnp.take(reduced, directions, axis=1)


def solution(mesh):
    placed = (
        P(None, None, "vec", "space", None),
        P(None, None, None, None, "space", None),
        P(),
        P(),
    )
    return jax.shard_map(
        on_device,
        mesh=mesh,
        in_specs=placed,
        out_specs=P(None, None, None, "space", "vec"),
        check_vma=False,
    )
```

profile of v0, /device:TPU:0, one launch (start us, length us, event | category | flops | bytes accessed | tf_op | source)
XLA Modules:
  0.0 521.4 jit_solution(13569363760980879944)
XLA Ops:
  6.5 0.7 all-gather.2.cloned.1.call-update
  7.3 0.0 all-reduce.3.cloned.1.call-start
  7.3 3.4 collective-permute-start
  10.7 0.7 slice_bitcast_fusion.2
  11.4 12.0 %copy.49 = f32[2,3,96,1,2048]{2,4,1,0,3:T(8,128)} copy(f32[2,3,96,1,2048]{4,3,2,1,0:T(1,128)} %param.4) | data formatting | bytes 9437184 | tf_op args[0]
  23.4 7.3 %slice.189 = f32[2,3,96,1,31,64]{2,5,4,1,0,3:T(8,128)} slice(f32[2,3,96,1,32,64]{2,5,4,1,0,3:T(8,128)} %bitcast.133), slice={[0:2], [0:3], [0:96], [0:1], [1:32], [0:64]} | slice | bytes 9142272 | tf_op jit(solution)/shard_map/jit(_roll_static)/slice | solution.py:32
  30.8 3.9 slice.193
  34.7 0.1 slice.194
  34.8 1.2 fusion.42
  36.0 0.1 copy_bitcast_fusion.14
  36.1 0.1 copy_bitcast_fusion.16
  36.2 3.6 fusion.41
  39.8 2.2 copy_bitcast_fusion.2
  42.0 11.1 %subtract_reduce_fusion.2 = (f32[3,96,2048]{2,1,0:T(8,128)}, f32[3,96,2048]{2,1,0:T(8,128)}, f32[3,96,2048]{2,1,0:T(8,128)}, f32[3,96,2048]{2,1,0:T(8,128)}) fusion(f32[3,96,2048]{2,1,0:T(8,128)S(1)} %get-tuple-element.50, f32[3,3,2048]{2,1,0:T(4,128)S(1)} %get-tuple-element.60, f32[3,96,2048]{2,1,0:T(8,128)S(1)} %get-tuple-element.51, ...), kind=kLoop, calls=%fused_computation.19 | loop fusion | flops 25952256 | bytes 14450688 | tf_op jit(solution)/shard_map/reduce_sum | solution.py:46
  53.1 2.2 copy.54
  55.4 3.6 copy.55
  59.0 6.9 %fusion.10 = (f32[1,3,96,1,32,64]{2,5,4,1,0,3:T(8,128)}, f32[1,3,96,1,32,64]{2,5,4,1,0,3:T(8,128)}) fusion(f32[2,3,96,1,31,64]{2,5,4,1,0,3:T(8,128)} %slice.189, f32[2,3,96,1,1,64]{2,5,4,1,0,3:T(8,128)S(1)} %slice.190), kind=kLoop, calls=%fused_computation.40 | loop fusion | flops 1179648 | bytes 9437184 | tf_op jit(solution)/shard_map/jit(_roll_static)/concatenate | solution.py:32
  65.9 3.4 copy.50
  69.3 3.4 copy.51
  72.7 3.5 copy.61
  76.2 3.5 copy.62
  79.7 7.0 %fusion.9 = (f32[1,3,96,1,32,64]{2,5,4,1,0,3:T(8,128)}, f32[1,3,96,1,32,64]{2,5,4,1,0,3:T(8,128)}) fusion(f32[2,3,96,1,32,63]{2,5,4,1,0,3:T(8,128)} %slice.193, f32[2,3,96,1,32,1]{2,5,4,1,0,3:T(1,128)S(1)} %slice.194), kind=kLoop, calls=%fused_computation.39 | loop fusion | flops 1179648 | bytes 9437184 | tf_op jit(solution)/shard_map/jit(_roll_static)/concatenate | solution.py:32
  86.7 3.4 copy.57
  90.1 3.4 copy.58
  93.5 0.2 multiply_reduce_fusion
  93.7 5.2 %fusion.8 = f32[2,3,96,1,32,64]{2,5,4,1,3,0:T(8,128)} fusion(f32[1,3,96,1,32,64]{2,5,4,1,3,0:T(8,128)} %bitcast.142, f32[1,3,96,1,32,64]{2,5,4,1,3,0:T(8,128)S(1)} %bitcast.141), kind=kLoop, calls=%fused_computation.30 | loop fusion | flops 3538944 | bytes 9437184 | tf_op jit(solution)/shard_map/jit(_roll_static)/concatenate | solution.py:32
  99.0 0.1 copy_bitcast_fusion.10
  99.1 0.1 copy_bitcast_fusion.8
  99.2 0.6 copy-done.3
  99.8 3.7 fusion.7
  103.5 0.1 copy_bitcast_fusion.12
  103.6 0.8 copy-done.7
  104.3 3.9 subtract_reduce_fusion.3
  108.3 4.7 subtract_reduce_fusion.1
  113.0 6.2 %copy.56 = f32[1,2,3,96,1,2048]{5,3,2,1,0,4:T(8,128)} copy(f32[1,2,3,96,1,2048]{3,5,2,1,4,0:T(8,128)} %bitcast.139) | data formatting | bytes 9437184 | tf_op jit(solution)/shard_map/reshape | solution.py:33
  119.2 6.6 %copy.63 = f32[1,2,3,96,1,2048]{5,3,2,1,0,4:T(8,128)} copy(f32[1,2,3,96,1,2048]{3,5,2,1,4,0:T(8,128)} %bitcast.140) | data formatting | bytes 9437184 | tf_op jit(solution)/shard_map/reshape | solution.py:33
  125.8 6.5 %maximum_subtract_fusion.1 = f32[1,2,3,96,1,2048]{5,3,2,1,0,4:T(8,128)} fusion(f32[1,2,3,96,1,2048]{5,3,2,1,0,4:T(8,128)} %copy.56, f32[1,1,3,96,1,2048]{5,3,2,1,0,4:T(8,128)} %bitcast.152, f32[1,1,3,96,1,2048]{5,3,2,1,0,4:T(8,128)S(1)} %bitcast.151), kind=kLoop, calls=%fused_computation.37 | loop fusion | flops 2359296 | bytes 14155776 | tf_op jit(solution)/shard_map/sub | solution.py:98
  132.4 0.5 copy-done.5
  132.9 3.0 maximum_subtract_fusion.2
  135.9 0.4 fusion.37
  136.3 1.0 slice_bitcast_fusion.3
  137.3 0.1 copy_bitcast_fusion.18
  137.4 6.4 %fusion.40 = (f32[1,3,96,1,2048]{4,3,2,1,0:T(1,128)S(1)}, f32[1,3,96,1,2048]{4,3,2,1,0:T(1,128)S(1)}) fusion(f32[2,3,96,1,2048]{4,3,2,1,0:T(1,128)} %collective-permute-done), kind=kLoop, calls=%fused_computation.124 | loop fusion | bytes 9437184 | tf_op jit(solution)/shard_map/slice | solution.py:44
  143.8 2.2 copy_bitcast_fusion.6
  146.1 2.8 subtract_reduce_fusion.5
  148.9 6.4 %fusion.39 = (f32[1,3,96,1,2048]{4,3,2,1,0:T(1,128)S(1)}, f32[1,3,96,1,2048]{4,3,2,1,0:T(1,128)S(1)}) fusion(f32[2,3,96,1,2048]{4,3,2,1,0:T(1,128)} %collective-permute-done.2), kind=kLoop, calls=%fused_computation.123 | loop fusion | bytes 9437184 | tf_op jit(solution)/shard_map/slice | solution.py:44
  155.3 2.2 copy_bitcast_fusion.4
  157.5 2.7 subtract_reduce_fusion.4
  160.2 3.0 maximum_subtract_fusion
  163.2 170.9 %all-gather.2.cloned.1.call-done = f32[2,3,384,1,2048]{4,3,2,1,0:T(1,128)} async-done(((f32[2,3,96,1,2048]{4,3,2,1,0:T(1,128)}), f32[2,3,384,1,2048]{4,3,2,1,0:T(1,128)}) %all-gather.2.cloned.1.call-update) | async-done | bytes 18874384 | tf_op jit(solution)/shard_map/all_gather | solution.py:104
  334.1 13.3 %fusion.38 = (f32[1,3,384,1,2048]{4,3,2,1,0:T(1,128)}, f32[1,3,384,1,2048]{4,3,2,1,0:T(1,128)}) fusion(f32[2,3,384,1,2048]{4,3,2,1,0:T(1,128)} %all-gather.2.cloned.1.call-done), kind=kLoop, calls=%fused_computation.122 | loop fusion | bytes 37748736 | tf_op jit(solution)/shard_map/slice | solution.py:65
  347.3 13.7 %copy_bitcast_fusion = (f32[3,384,2048]{2,1,0:T(8,128)S(1)}, f32[3,384,2048]{2,1,0:T(8,128)S(1)}) fusion(f32[1,3,384,1,2048]{4,3,2,1,0:T(1,128)} %get-tuple-element.25, f32[1,3,384,1,2048]{4,3,2,1,0:T(1,128)} %get-tuple-element.24), kind=kLoop, calls=%fused_computation.12 | loop fusion | bytes 37748736
  361.0 13.2 %multiply_subtract_fusion = (f32[2,1,3,384,1,2048]{5,3,2,1,0,4:T(8,128)}, f32[2,1,3,384,1,2048]{5,3,2,1,0,4:T(8,128)}) fusion(f32[2,2048]{1,0:T(2,128)S(1)} %get-tuple-element.49, f32[3,384,2048]{2,1,0:T(8,128)S(1)} %get-tuple-element.70, f32[2,2048]{1,0:T(2,128)S(1)} %get-tuple-element.48, f32[3,384,2048]{2,1,0:T(8,128)S(1)} %get-tuple-element.71), kind=kLoop, calls=%fused_computation.6 | loop fusion | flops 33030144 | bytes 56655872 | tf_op jit(solution)/shard_map/sub | solution.py:69
  374.2 71.7 %fusion.11 = f32[2,2,384,3,2,96]{2,5,4,3,1,0:T(8,128)S(1)} fusion(f32[1,2,3,96,1,2048]{5,3,2,1,0,4:T(8,128)} %maximum_subtract_fusion.2, f32[1,2,3,96,1,2048]{5,3,2,1,0,4:T(8,128)} %maximum_subtract_fusion.1, f32[1,2,3,96,1,2048]{5,3,2,1,0,4:T(8,128)} %maximum_subtract_fusion, f32[2,1,3,384,1,2048]{5,3,2,1,0,4:T(8,128)} %get-tuple-element.23, ...), kind=kOutput, calls=%fused_computation.49 | convolution fusion | flops 65246330880 | bytes 55443456 | tf_op jit(solution)/shard_map/mpcaxs,dqcbxs->mpadqb/dot_general | solution.py:72
  445.9 0.1 fusion.12
  446.0 0.1 fusion.14
  446.1 0.1 maximum_bitcast_fusion.8
  446.3 3.1 copy.66
  449.4 0.6 dynamic-slice
  450.7 60.5 %all-reduce.3.cloned.1.call-done = f32[2,3,2,384,96]{4,2,1,0,3:T(2,128)} async-done(((f32[2,3,2,384,96]{4,2,1,0,3:T(2,128)}), f32[2,3,2,384,96]{4,2,1,0,3:T(2,128)}) %all-reduce.3.cloned.1.call-update) | async-done | bytes 1769488
  511.3 1.0 constant_dynamic-slice_fusion
  512.3 0.9 gather_fusion
  513.2 0.2 select_bitcast_fusion
  513.4 0.7 copy.67
  (53 shorter events, 0.2 us)
Async XLA Ops:
  6.5 4.2 copy-start.10
  6.5 327.5 %all-gather.2.cloned.1.call-start = ((), (), s32[]{:S(2)}) async-start(), calls=%async_computation | async-start | bytes 23592960 | tf_op jit(solution)/shard_map/all_gather | solution.py:104
  7.3 504.0 %all-reduce.3.cloned.1.call-start = ((), (), s32[]{:S(2)}) async-start(), calls=%async_computation.1 | async-start | bytes 4718592
  7.3 130.1 %collective-permute-start = (f32[2,3,96,1,2048]{4,3,2,1,0:T(1,128)}, f32[2,3,96,1,2048]{4,3,2,1,0:T(1,128)}, u32[]{:S(2)}, u32[]{:S(2)}) collective-permute-start(f32[2,3,96,1,2048]{4,3,2,1,0:T(1,128)} %param.4), channel_id=1, source_target_pairs={{4,0},{8,4},{12,8},{16,12},{20,16},{24,20},{28,24},{0,28},{5,1},{9... | collective-permute-start | bytes 14155784 | tf_op jit(solution)/shard_map/ppermute | solution.py:18
  10.7 138.1 %collective-permute-start.2 = (f32[2,3,96,1,2048]{4,3,2,1,0:T(1,128)}, f32[2,3,96,1,2048]{4,3,2,1,0:T(1,128)}, u32[]{:S(2)}, u32[]{:S(2)}) collective-permute-start(f32[2,3,96,1,2048]{4,3,2,1,0:T(1,128)} %param.4), channel_id=1, source_target_pairs={{0,4},{4,8},{8,12},{12,16},{16,20},{20,24},{24,28},{28,0},{1,5},{5... | collective-permute-start | bytes 14155784 | tf_op jit(solution)/shard_map/ppermute | solution.py:17
  11.4 124.9 %collective-permute-start.1 = (f32[2,3,3,1,2048]{4,3,2,1,0:T(1,128)}, f32[2,3,3,1,2048]{4,3,2,1,0:T(1,128)}, u32[]{:S(2)}, u32[]{:S(2)}) collective-permute-start(f32[2,3,3,1,2048]{4,3,2,1,0:T(1,128)} %slice_bitcast_fusion.2), channel_id=1, source_target_pairs={{0,4},{4,8},{8,12},{12,16},{16,20},{20,24},{24,28},{28,0},{1,5},{5... | collective-permute-start | bytes 442376 | tf_op jit(solution)/shard_map/ppermute | solution.py:26
  23.4 7.3 %copy-start = (f32[2,3,96,1,2048]{2,4,1,0,3:T(8,128)S(1)}, f32[2,3,96,1,2048]{2,4,1,0,3:T(8,128)}, u32[]{:S(2)}) copy-start(f32[2,3,96,1,2048]{2,4,1,0,3:T(8,128)} %copy.49) | copy-start | bytes 14155780
  30.8 5.4 %slice-start = ((s8[4718592]{0:T(1024)(128)(4,1)}), s8[4194304]{0:T(1024)(128)(4,1)S(1)}, s32[]{:S(2)}) async-start(s8[4718592]{0:T(1024)(128)(4,1)} %bitcast.137), calls=%async_computation.2 | async-start | bytes 8388608
  30.8 5.4 %slice-start.1 = ((s8[4718592]{0:T(1024)(128)(4,1)}), s8[524288]{0:T(1024)(128)(4,1)S(1)}, s32[]{:S(2)}) async-start(s8[4718592]{0:T(1024)(128)(4,1)} %bitcast.137), calls=%async_computation.3 | async-start | bytes 1048576
  86.7 6.8 %copy-start.16 = (s32[2,3]{1,0:T(2,128)S(1)}, s32[2,3]{1,0:T(2,128)}, u32[]{:S(2)}) copy-start(s32[2,3]{1,0:T(2,128)} %param.6) | copy-start | bytes 76
  93.7 5.3 %copy-start.14 = (f32[1,1,3,3,1,2048]{5,4,3,2,1,0:T(1,128)S(1)}, f32[1,1,3,3,1,2048]{5,4,3,2,1,0:T(1,128)}, u32[]{:S(2)}) copy-start(f32[1,1,3,3,1,2048]{5,4,3,2,1,0:T(1,128)} %get-tuple-element.41) | copy-start | bytes 221188
  93.7 5.3 %copy-start.15 = (f32[1,1,3,3,1,2048]{5,4,3,2,1,0:T(1,128)S(1)}, f32[1,1,3,3,1,2048]{5,4,3,2,1,0:T(1,128)}, u32[]{:S(2)}) copy-start(f32[1,1,3,3,1,2048]{5,4,3,2,1,0:T(1,128)} %get-tuple-element.42) | copy-start | bytes 221188
  93.7 5.4 %copy-start.12 = (f32[1,1,3,3,1,2048]{5,4,3,2,1,0:T(1,128)S(1)}, f32[1,1,3,3,1,2048]{5,4,3,2,1,0:T(1,128)}, u32[]{:S(2)}) copy-start(f32[1,1,3,3,1,2048]{5,4,3,2,1,0:T(1,128)} %get-tuple-element.44) | copy-start | bytes 221188
  93.7 5.4 %copy-start.13 = (f32[1,1,3,3,1,2048]{5,4,3,2,1,0:T(1,128)S(1)}, f32[1,1,3,3,1,2048]{5,4,3,2,1,0:T(1,128)}, u32[]{:S(2)}) copy-start(f32[1,1,3,3,1,2048]{5,4,3,2,1,0:T(1,128)} %get-tuple-element.45) | copy-start | bytes 221188
  93.7 5.5 %copy-start.2 = (f32[3,96,2048]{1,2,0:T(8,128)S(1)}, f32[3,96,2048]{1,2,0:T(8,128)}, u32[]{:S(2)}) copy-start(f32[3,96,2048]{1,2,0:T(8,128)} %copy.61) | copy-start | bytes 7077892
  93.7 6.0 %copy-start.3 = (f32[3,96,2048]{1,2,0:T(8,128)S(1)}, f32[3,96,2048]{1,2,0:T(8,128)}, u32[]{:S(2)}) copy-start(f32[3,96,2048]{1,2,0:T(8,128)} %copy.62) | copy-start | bytes 7077892
  99.8 3.7 copy-start.11
  99.8 3.8 copy-start.6
  99.8 4.6 copy-start.7
  104.3 3.9 copy-start.8
  104.3 3.9 copy-start.9
  125.8 6.6 %copy-start.1 = (f32[1,2,3,96,1,2048]{5,3,2,1,0,4:T(8,128)S(1)}, f32[1,2,3,96,1,2048]{5,3,2,1,0,4:T(8,128)}, u32[]{:S(2)}) copy-start(f32[1,2,3,96,1,2048]{5,3,2,1,0,4:T(8,128)} %copy.63) | copy-start | bytes 14155780
  125.8 6.6 %copy-start.4 = (f32[3,96,2048]{2,1,0:T(8,128)S(1)}, f32[3,96,2048]{2,1,0:T(8,128)}, u32[]{:S(2)}) copy-start(f32[3,96,2048]{2,1,0:T(8,128)} %get-tuple-element.13) | copy-start | bytes 7077892
  125.8 7.1 %copy-start.5 = (f32[3,96,2048]{2,1,0:T(8,128)S(1)}, f32[3,96,2048]{2,1,0:T(8,128)}, u32[]{:S(2)}) copy-start(f32[3,96,2048]{2,1,0:T(8,128)} %get-tuple-element.14) | copy-start | bytes 7077892
  446.1 3.3 copy-start.18
  446.1 4.6 copy-start.17
Sparse Core Ops, SparseCore 0:
  8.9 325.1 all-gather.1
  449.6 61.6 all-reduce.2
where the time goes:
time: 531 us; the launch traced here: 521 us
  waiting for transfers between devices  232 us (44%)
  local copies, waits for them, and re-layouts  122 us (23%)
  other arithmetic  77.1 us (15%)
  matrix products  71.7 us (14%)
  between operations  14.8 us (3%)
    all_gather x1, waiting for transfers between devices, on_device(): lax.all_gather(vectors, 'vec', axis=2, tiled=True)  171 us
    dot_general x1, matrix products, elemental_block(): jnp.einsum('mpcaxs,dqcbxs->mpadqb', left, right_disp, precision=lax.Preci...  71.7 us
    unnamed x3, waiting for transfers between devices  61.3 us
    unnamed x52, local copies, waits for them, and re-layouts  36.2 us
    reduce_sum x5, other arithmetic, color_apply(): out_re = jnp.sum(link_re * field_re - link_im * field_im, axis=1)  25.2 us
    concatenate x4, other arithmetic, site_shift(): cube = jnp.roll(cube, -step, axis=-3 + mu)  22.9 us
    slice x3, local copies, waits for them, and re-layouts, color_apply(): field_re = field[0][None]  16.5 us
    mul x7, local copies, waits for them, and re-layouts, color_apply(): out_re = jnp.sum(link_re * field_re - link_im * field_im, axis=1)  13.8 us
  transfers between devices with their start and end apart: 5, of which 2 were waited for; matrix products, arithmetic and copies ran while one was open for 29% of the time, Pallas kernels for 0%

commit v1 on v0

--- a/solution.py
+++ b/solution.py
@@ -5,6 +5,27 @@
 
 LY = 32
 LZ = 64
+
+
+def collect(x, axis, dim):
+    peers, here, rows = (lax.axis_size(axis), lax.axis_index(axis), x.shape[dim])
+    upward = [(i, (i + 1) % peers) for i in range(peers)]
+    behind = [(i, (i - 1) % peers) for i in range(peers)]
+    filled = jnp.zeros((*x.shape[:dim], peers * rows, *x.shape[dim + 1 :]), x.dtype)
+    filled = lax.dynamic_update_slice_in_dim(filled, x, here * rows, axis=dim)
+    from_left = from_right = x
+    middle = peers // 2
+    for step in range(1, middle + 1):
+        from_left = lax.ppermute(from_left, axis, upward)
+        filled = lax.dynamic_update_slice_in_dim(
+            filled, from_left, (here - step) % peers * rows, axis=dim
+        )
+        if step < peers - middle:
+            from_right = lax.ppermute(from_right, axis, behind)
+            filled = lax.dynamic_update_slice_in_dim(
+                filled, from_right, (here + step) % peers * rows, axis=dim
+            )
+    return filled
 
 
 def padded_2(shard, sides, width):
@@ -100,9 +121,7 @@
     site_count = vectors.shape[4]
     sites = jnp.arange(site_count, dtype=jnp.int32)
     cosine, sine = phase_tables(momenta, xcoord, sites, extent_x, plane_y, plane_z)
-    block = elemental_block(
-        lax.all_gather(vectors, "vec", axis=2, tiled=True), displaced, cosine, sine
-    )
+    block = elemental_block(collect(vectors, "vec", 2), displaced, cosine, sine)
     reduced = lax.psum_scatter(block, "space", scatter_dimension=3, tiled=True)
     return jnp.take(reduced, directions, axis=1)
 

time: 531 us -> 493 us (0.928); the launches traced: 521 us -> 489 us
  waiting for transfers between devices: 232 us -> 184 us
  local copies, waits for them, and re-layouts: 122 us -> 138 us
    all_gather x1 -> x0, waiting for transfers between devices: 171 us -> none  [on_device(): lax.all_gather(vectors, 'vec', axis=2, tiled=True)]
    ppermute x0 -> x3, waiting for transfers between devices: none -> 123 us  [the longest x2 94.7 us: collect(): from_left = lax.ppermute(from_left, axis, upward)]
    dynamic_update_slice x0 -> x4, local copies, waits for them, and re-layouts: none -> 22.2 us  [the longest x2 11.1 us: collect(): lax.dynamic_update_slice_in_dim(filled, from_left, (here - step) % peers...]
    slice x1 -> x0, local copies, waits for them, and re-layouts: 13.3 us -> none  [elemental_block(): vec_re = left_vecs[0][None]]
    unnamed x52 -> x55, local copies, waits for them, and re-layouts: 36.2 us -> 24.6 us
    broadcast_in_dim x0 -> x1, local copies, waits for them, and re-layouts: none -> 8.87 us  [collect(): jnp.zeros((*x.shape[:dim], peers * rows, *x.shape[dim + 1:]), x.dtype)]
    mul x0 -> x1, local copies, waits for them, and re-layouts: none -> 7.21 us  [elemental_block(): left_re = vec_re * cosine - vec_im * sine]
    concatenate x4, other arithmetic: 22.9 us -> 16 us  [site_shift(): cube = jnp.roll(cube, -step, axis=-3 + mu)]
  transfers between devices with their start and end apart: 5 -> 7, of which waited for: 2 -> 3; matrix products, arithmetic and copies ran while one was open for 29% -> 36% of each run, Pallas kernels for 0% -> 0%
where the time goes in v1:
time: 493 us; the launch traced here: 489 us
  waiting for transfers between devices  184 us (37%)
  local copies, waits for them, and re-layouts  138 us (28%)
  other arithmetic  72.5 us (15%)
  matrix products  71.7 us (15%)
  between operations  14.9 us (3%)
  starting transfers between devices  7.43 us (2%)
    ppermute x2, waiting for transfers between devices, collect(): from_left = lax.ppermute(from_left, axis, upward)  94.7 us
    dot_general x1, matrix products, elemental_block(): jnp.einsum('mpcaxs,dqcbxs->mpadqb', left, right_disp, precision=lax.Preci...  71.7 us
    unnamed x2, waiting for transfers between devices  61.2 us
    ppermute x1, waiting for transfers between devices, collect(): from_right = lax.ppermute(from_right, axis, behind)  28.3 us
    reduce_sum x5, other arithmetic, color_apply(): out_re = jnp.sum(link_re * field_re - link_im * field_im, axis=1)  26.3 us
    unnamed x55, local copies, waits for them, and re-layouts  24.6 us
    slice x3, local copies, waits for them, and re-layouts, color_apply(): field_re = field[0][None]  21 us
    concatenate x4, other arithmetic, site_shift(): cube = jnp.roll(cube, -step, axis=-3 + mu)  16 us
  transfers between devices with their start and end apart: 7, of which 3 were waited for; matrix products, arithmetic and copies ran while one was open for 36% of the time, Pallas kernels for 0%

profile of v1, /device:TPU:0, one launch (start us, length us, event | category | flops | bytes accessed | tf_op | source)
XLA Modules:
  0.0 488.8 jit_solution(3058985636810327286)
XLA Ops:
  6.5 3.1 collective-permute-start
  9.6 2.0 collective-permute-start.1
  11.6 1.6 collective-permute-start.3
  13.2 1.6 slice_bitcast_fusion.4
  14.8 0.2 collective-permute-start.4
  15.0 2.2 fusion.41
  17.2 8.2 %fusion.40 = (f32[1,3,96,1,2048]{4,3,2,1,0:T(1,128)S(1)}, f32[1,3,96,1,2048]{4,3,2,1,0:T(1,128)}) fusion(f32[2,3,96,1,2048]{4,3,2,1,0:T(1,128)} %param.4), kind=kLoop, calls=%fused_computation.128 | loop fusion | bytes 9437184 | tf_op jit(solution)/shard_map/slice | solution.py:65
  25.4 11.9 %copy.65 = f32[2,3,96,1,2048]{2,4,1,0,3:T(8,128)} copy(f32[2,3,96,1,2048]{4,3,2,1,0:T(1,128)} %param.4) | data formatting | bytes 9437184 | tf_op args[0]
  37.3 6.5 %slice.189 = f32[2,3,96,1,31,64]{2,5,4,1,0,3:T(8,128)} slice(f32[2,3,96,1,32,64]{2,5,4,1,0,3:T(8,128)} %bitcast.133), slice={[0:2], [0:3], [0:96], [0:1], [1:32], [0:64]} | slice | bytes 9142272 | tf_op jit(solution)/shard_map/jit(_roll_static)/slice | solution.py:53
  43.9 3.5 slice.193
  47.4 0.1 slice.194
  47.7 3.9 copy_bitcast_fusion
  51.6 10.3 %subtract_reduce_fusion.2 = (f32[3,96,2048]{2,1,0:T(8,128)}, f32[3,96,2048]{2,1,0:T(8,128)}, f32[3,96,2048]{2,1,0:T(8,128)}, f32[3,96,2048]{2,1,0:T(8,128)S(1)}) fusion(f32[3,96,2048]{2,1,0:T(8,128)S(1)} %get-tuple-element.50, f32[3,3,2048]{2,1,0:T(4,128)S(1)} %get-tuple-element.60, f32[3,96,2048]{2,1,0:T(8,128)S(1)} %get-tuple-element.51, ...), kind=kLoop, calls=%fused_computation.19 | loop fusion | flops 25952256 | bytes 14450688 | tf_op jit(solution)/shard_map/reduce_sum | solution.py:67
  61.9 3.5 copy.70
  65.3 3.5 copy.71
  68.8 2.3 copy.77
  71.1 3.5 copy.78
  74.7 0.2 multiply_reduce_fusion
  74.9 5.4 %fusion.8 = f32[2,3,96,1,32,64]{2,5,4,1,3,0:T(8,128)} fusion(f32[1,3,96,1,32,64]{2,5,4,1,3,0:T(8,128)} %bitcast.152, f32[1,3,96,1,32,64]{2,5,4,1,3,0:T(8,128)} %bitcast.151), kind=kLoop, calls=%fused_computation.30 | loop fusion | flops 3538944 | bytes 9437184 | tf_op jit(solution)/shard_map/jit(_roll_static)/concatenate | solution.py:53
  80.4 3.9 fusion.10
  84.3 1.2 copy-done.5
  85.5 3.2 fusion.7
  88.7 0.8 copy_bitcast_fusion.6
  89.5 3.5 fusion.9
  93.1 3.6 copy.66
  96.7 2.5 copy.67
  99.2 3.6 copy.73
  102.8 2.2 copy.74
  105.1 5.7 %subtract_reduce_fusion.3 = (f32[3,96,2048]{2,1,0:T(8,128)S(1)}, f32[3,96,2048]{2,1,0:T(8,128)}) fusion(f32[3,96,2048]{2,1,0:T(8,128)} %copy.67, f32[3,3,2048]{2,1,0:T(4,128)S(1)} %get-tuple-element.54, f32[3,96,2048]{2,1,0:T(8,128)} %copy.66, f32[3,3,2048]{2,1,0:T(4,128)S(1)} %get-tuple-element.55), kind=kLoop, calls=%fused_computation.21 | loop fusion | flops 12976128 | bytes 9584640 | tf_op jit(solution)/shard_map/reduce_sum | solution.py:67
  110.8 4.7 subtract_reduce_fusion.1
  115.5 8.9 %broadcast_in_dim.12 = f32[2,3,384,1,2048]{4,2,1,3,0:T(8,128)} broadcast(f32[]{:T(128)} %constant.109.clone.1), dimensions={} | broadcast | bytes 18874372 | tf_op jit(solution)/shard_map/broadcast_in_dim | solution.py:14
  124.3 4.4 copy_dynamic-update-slice_fusion.3
  128.7 6.3 %copy.72 = f32[1,2,3,96,1,2048]{5,3,2,1,0,4:T(8,128)} copy(f32[1,2,3,96,1,2048]{3,5,2,1,4,0:T(8,128)} %bitcast.141) | data formatting | bytes 9437184 | tf_op jit(solution)/shard_map/reshape | solution.py:54
  135.0 6.2 %copy.79 = f32[1,2,3,96,1,2048]{5,3,2,1,0,4:T(8,128)} copy(f32[1,2,3,96,1,2048]{3,5,2,1,4,0:T(8,128)} %bitcast.142) | data formatting | bytes 9437184 | tf_op jit(solution)/shard_map/reshape | solution.py:54
  141.2 6.5 %maximum_subtract_fusion.1 = f32[1,2,3,96,1,2048]{5,3,2,1,0,4:T(8,128)} fusion(f32[1,2,3,96,1,2048]{5,3,2,1,0,4:T(8,128)} %copy.72, f32[1,1,3,96,1,2048]{5,3,2,1,0,4:T(8,128)} %bitcast.156, f32[1,1,3,96,1,2048]{5,3,2,1,0,4:T(8,128)S(1)} %bitcast.155), kind=kLoop, calls=%fused_computation.37 | loop fusion | flops 2359296 | bytes 14155776 | tf_op jit(solution)/shard_map/sub | solution.py:119
  147.7 0.6 copy-done.7
  148.3 3.1 maximum_subtract_fusion.2
  151.4 0.4 fusion.37
  151.9 1.0 slice_bitcast_fusion.5
  153.0 0.5 collective-permute-start.2
  153.5 6.4 %fusion.39 = (f32[1,3,96,1,2048]{4,3,2,1,0:T(1,128)S(1)}, f32[1,3,96,1,2048]{4,3,2,1,0:T(1,128)S(1)}) fusion(f32[2,3,96,1,2048]{4,3,2,1,0:T(1,128)} %collective-permute-done.3), kind=kLoop, calls=%fused_computation.127 | loop fusion | bytes 9437184 | tf_op jit(solution)/shard_map/slice | solution.py:65
  159.9 2.2 copy_bitcast_fusion.4
  162.1 2.8 subtract_reduce_fusion.5
  164.9 6.4 %fusion.38 = (f32[1,3,96,1,2048]{4,3,2,1,0:T(1,128)S(1)}, f32[1,3,96,1,2048]{4,3,2,1,0:T(1,128)S(1)}) fusion(f32[2,3,96,1,2048]{4,3,2,1,0:T(1,128)} %collective-permute-done.5), kind=kLoop, calls=%fused_computation.126 | loop fusion | bytes 9437184 | tf_op jit(solution)/shard_map/slice | solution.py:65
  171.3 2.2 copy_bitcast_fusion.2
  173.6 2.9 subtract_reduce_fusion.4
  176.5 3.0 maximum_subtract_fusion
  179.5 6.7 %copy_dynamic-update-slice_fusion.2 = f32[2,3,384,1,2048]{4,2,1,3,0:T(8,128)} fusion(f32[2,3,384,1,2048]{4,2,1,3,0:T(8,128)} %copy_dynamic-update-slice_fusion.3, s32[]{:T(128)S(6)} %select_n.99, f32[2,3,96,1,2048]{4,3,2,1,0:T(1,128)} %collective-permute-done), kind=kLoop, calls=%fused_computation.41 | loop fusion | bytes 9437188 | tf_op jit(solution)/shard_map/dynamic_update_slice | solution.py:20
  186.2 28.3 %collective-permute-done.1 = f32[2,3,96,1,2048]{4,3,2,1,0:T(1,128)} collective-permute-done((f32[2,3,96,1,2048]{4,3,2,1,0:T(1,128)}, f32[2,3,96,1,2048]{4,3,2,1,0:T(1,128)}, u32[]{:S(2)}, u32[]{:S(2)}) %collective-permute-start.1) | collective-permute-done | bytes 4718624 | tf_op jit(solution)/shard_map/ppermute | solution.py:24
  214.5 6.7 %copy_dynamic-update-slice_fusion.1 = f32[2,3,384,1,2048]{4,2,1,3,0:T(8,128)} fusion(f32[2,3,384,1,2048]{4,2,1,3,0:T(8,128)} %copy_dynamic-update-slice_fusion.2, s32[]{:T(128)S(6)} %select_n.101, f32[2,3,96,1,2048]{4,3,2,1,0:T(1,128)} %collective-permute-done.1), kind=kLoop, calls=%fused_computation.40 | loop fusion | bytes 9437188 | tf_op jit(solution)/shard_map/dynamic_update_slice | solution.py:25
  221.2 94.7 %collective-permute-done.2 = f32[2,3,96,1,2048]{4,3,2,1,0:T(1,128)S(1)} collective-permute-done((f32[2,3,96,1,2048]{4,3,2,1,0:T(1,128)}, f32[2,3,96,1,2048]{4,3,2,1,0:T(1,128)S(1)}, u32[]{:S(2)}, u32[]{:S(2)}) %collective-permute-start.2) | collective-permute-done | bytes 4718624 | tf_op jit(solution)/shard_map/ppermute | solution.py:19
  315.9 4.4 copy_dynamic-update-slice_fusion
  320.3 7.2 %slice_bitcast_fusion.1 = (f32[3,384,2048]{2,1,0:T(8,128)S(1)}, f32[3,384,2048]{2,1,0:T(8,128)S(1)}) fusion(f32[2,3,384,1,2048]{4,2,1,3,0:T(8,128)} %copy_dynamic-update-slice_fusion), kind=kLoop, calls=%fused_computation.13 | loop fusion | bytes 37748736 | tf_op jit(solution)/shard_map/mul | solution.py:90
  327.5 13.3 %multiply_subtract_fusion = (f32[2,1,3,384,1,2048]{5,3,2,1,0,4:T(8,128)}, f32[2,1,3,384,1,2048]{5,3,2,1,0,4:T(8,128)}) fusion(f32[2,2048]{1,0:T(2,128)S(1)} %get-tuple-element.49, f32[3,384,2048]{2,1,0:T(8,128)S(1)} %get-tuple-element.25, f32[2,2048]{1,0:T(2,128)S(1)} %get-tuple-element.48, f32[3,384,2048]{2,1,0:T(8,128)S(1)} %get-tuple-element.24), kind=kLoop, calls=%fused_computation.6 | loop fusion | flops 33030144 | bytes 56655872 | tf_op jit(solution)/shard_map/sub | solution.py:90
  340.8 71.7 %fusion.11 = f32[2,2,384,3,2,96]{2,5,4,3,1,0:T(8,128)S(1)} fusion(f32[1,2,3,96,1,2048]{5,3,2,1,0,4:T(8,128)} %maximum_subtract_fusion.2, f32[1,2,3,96,1,2048]{5,3,2,1,0,4:T(8,128)} %maximum_subtract_fusion.1, f32[1,2,3,96,1,2048]{5,3,2,1,0,4:T(8,128)} %maximum_subtract_fusion, f32[2,1,3,384,1,2048]{5,3,2,1,0,4:T(8,128)} %get-tuple-element.23, ...), kind=kOutput, calls=%fused_computation.53 | convolution fusion | flops 65246330880 | bytes 55443456 | tf_op jit(solution)/shard_map/mpcaxs,dqcbxs->mpadqb/dot_general | solution.py:93
  412.5 0.1 fusion.12
  412.7 0.1 maximum_bitcast_fusion.8
  412.8 3.2 copy.82
  416.1 0.6 dynamic-slice
  417.4 61.2 %all-reduce.3.cloned.1.call-done = f32[2,3,2,384,96]{4,2,1,0,3:T(2,128)} async-done(((f32[2,3,2,384,96]{4,2,1,0,3:T(2,128)}), f32[2,3,2,384,96]{4,2,1,0,3:T(2,128)}) %all-reduce.3.cloned.1.call-update) | async-done | bytes 1769488
  478.6 1.0 constant_dynamic-slice_fusion
  479.6 0.9 gather_fusion
  480.5 0.2 select_bitcast_fusion
  480.7 0.7 copy.83
  (66 shorter events, 0.7 us)
Async XLA Ops:
  6.5 472.0 %all-reduce.3.cloned.1.call-start = ((), (), s32[]{:S(2)}) async-start(), calls=%async_computation | async-start | bytes 4718592
  6.5 146.4 %collective-permute-start = (f32[2,3,96,1,2048]{4,3,2,1,0:T(1,128)}, f32[2,3,96,1,2048]{4,3,2,1,0:T(1,128)}, u32[]{:S(2)}, u32[]{:S(2)}) collective-permute-start(f32[2,3,96,1,2048]{4,3,2,1,0:T(1,128)} %param.4), channel_id=1, source_target_pairs={{0,1},{1,2},{2,3},{3,0},{4,5},{5,6},{6,7},{7,4},{8,9},{9,10},{10,1... | collective-permute-start | bytes 14155784 | tf_op jit(solution)/shard_map/ppermute | solution.py:19
  9.6 204.9 %collective-permute-start.1 = (f32[2,3,96,1,2048]{4,3,2,1,0:T(1,128)}, f32[2,3,96,1,2048]{4,3,2,1,0:T(1,128)}, u32[]{:S(2)}, u32[]{:S(2)}) collective-permute-start(f32[2,3,96,1,2048]{4,3,2,1,0:T(1,128)} %param.4), channel_id=1, source_target_pairs={{0,3},{1,0},{2,1},{3,2},{4,7},{5,4},{6,5},{7,6},{8,11},{9,8},{10,9... | collective-permute-start | bytes 14155784 | tf_op jit(solution)/shard_map/ppermute | solution.py:24
  11.6 141.9 %collective-permute-start.3 = (f32[2,3,96,1,2048]{4,3,2,1,0:T(1,128)}, f32[2,3,96,1,2048]{4,3,2,1,0:T(1,128)}, u32[]{:S(2)}, u32[]{:S(2)}) collective-permute-start(f32[2,3,96,1,2048]{4,3,2,1,0:T(1,128)} %param.4), channel_id=1, source_target_pairs={{4,0},{8,4},{12,8},{16,12},{20,16},{24,20},{28,24},{0,28},{5,1},{9... | collective-permute-start | bytes 14155784 | tf_op jit(solution)/shard_map/ppermute | solution.py:39
  13.2 151.7 %collective-permute-start.5 = (f32[2,3,96,1,2048]{4,3,2,1,0:T(1,128)}, f32[2,3,96,1,2048]{4,3,2,1,0:T(1,128)}, u32[]{:S(2)}, u32[]{:S(2)}) collective-permute-start(f32[2,3,96,1,2048]{4,3,2,1,0:T(1,128)} %param.4), channel_id=1, source_target_pairs={{0,4},{4,8},{8,12},{12,16},{16,20},{20,24},{24,28},{28,0},{1,5},{5... | collective-permute-start | bytes 14155784 | tf_op jit(solution)/shard_map/ppermute | solution.py:38
  14.8 137.1 %collective-permute-start.4 = (f32[2,3,3,1,2048]{4,3,2,1,0:T(1,128)}, f32[2,3,3,1,2048]{4,3,2,1,0:T(1,128)}, u32[]{:S(2)}, u32[]{:S(2)}) collective-permute-start(f32[2,3,3,1,2048]{4,3,2,1,0:T(1,128)} %slice_bitcast_fusion.4), channel_id=1, source_target_pairs={{0,4},{4,8},{8,12},{12,16},{16,20},{20,24},{24,28},{28,0},{1,5},{5... | collective-permute-start | bytes 442376 | tf_op jit(solution)/shard_map/ppermute | solution.py:47
  37.3 6.5 %copy-start = (f32[2,3,96,1,2048]{2,4,1,0,3:T(8,128)S(1)}, f32[2,3,96,1,2048]{2,4,1,0,3:T(8,128)}, u32[]{:S(2)}) copy-start(f32[2,3,96,1,2048]{2,4,1,0,3:T(8,128)} %copy.65) | copy-start | bytes 14155780
  68.8 5.9 %copy-start.14 = (s32[2,3]{1,0:T(2,128)S(1)}, s32[2,3]{1,0:T(2,128)}, u32[]{:S(2)}) copy-start(s32[2,3]{1,0:T(2,128)} %param.6) | copy-start | bytes 76
  71.1 9.2 %slice-start.4 = ((s8[6094848]{0:T(1024)(128)(4,1)}), s8[1900544]{0:T(1024)(128)(4,1)S(1)}, s32[]{:S(2)}) async-start(s8[6094848]{0:T(1024)(128)(4,1)} %bitcast.143), calls=%async_computation.5 | async-start | bytes 3801088
  74.9 5.5 %slice-start.5 = ((s8[6094848]{0:T(1024)(128)(4,1)}), s8[4194304]{0:T(1024)(128)(4,1)S(1)}, s32[]{:S(2)}) async-start(s8[6094848]{0:T(1024)(128)(4,1)} %bitcast.143), calls=%async_computation.6 | async-start | bytes 8388608
  80.4 4.0 copy-start.4
  80.4 5.1 %copy-start.5 = (f32[3,96,2048]{1,2,0:T(8,128)S(1)}, f32[3,96,2048]{1,2,0:T(8,128)}, u32[]{:S(2)}) copy-start(f32[3,96,2048]{1,2,0:T(8,128)} %copy.78) | copy-start | bytes 7077892
  80.4 9.1 %slice-start.2 = ((s8[6291456]{0:T(1024)(128)(4,1)}), s8[4194304]{0:T(1024)(128)(4,1)S(1)}, s32[]{:S(2)}) async-start(s8[6291456]{0:T(1024)(128)(4,1)} %bitcast.139), calls=%async_computation.3 | async-start | bytes 8388608
  85.5 4.0 slice-start.3
  89.5 3.5 copy-start.12
  89.5 3.5 copy-start.13
  93.0 3.7 copy-start.2
  99.2 3.6 copy-start.3
  105.1 5.7 %copy-start.8 = (f32[3,96,2048]{2,1,0:T(8,128)S(1)}, f32[3,96,2048]{2,1,0:T(8,128)}, u32[]{:S(2)}) copy-start(f32[3,96,2048]{2,1,0:T(8,128)} %copy.73) | copy-start | bytes 7077892
  105.1 5.7 %copy-start.9 = (f32[3,96,2048]{2,1,0:T(8,128)S(1)}, f32[3,96,2048]{2,1,0:T(8,128)}, u32[]{:S(2)}) copy-start(f32[3,96,2048]{2,1,0:T(8,128)} %copy.74) | copy-start | bytes 7077892
  105.1 5.7 %copy-start.10 = (f32[3,3,2048]{2,1,0:T(4,128)S(1)}, f32[3,3,2048]{2,1,0:T(4,128)}, u32[]{:S(2)}) copy-start(f32[3,3,2048]{2,1,0:T(4,128)} %get-tuple-element.52) | copy-start | bytes 221188
  105.1 5.7 %copy-start.11 = (f32[3,3,2048]{2,1,0:T(4,128)S(1)}, f32[3,3,2048]{2,1,0:T(4,128)}, u32[]{:S(2)}) copy-start(f32[3,3,2048]{2,1,0:T(4,128)} %get-tuple-element.53) | copy-start | bytes 221188
  110.8 13.6 %slice-start = ((s8[4718592]{0:T(1024)(128)(4,1)}), s8[4194304]{0:T(1024)(128)(4,1)S(1)}, s32[]{:S(2)}) async-start(s8[4718592]{0:T(1024)(128)(4,1)} %bitcast.137), calls=%async_computation.1 | async-start | bytes 8388608
  115.5 8.9 %slice-start.1 = ((s8[4718592]{0:T(1024)(128)(4,1)}), s8[524288]{0:T(1024)(128)(4,1)S(1)}, s32[]{:S(2)}) async-start(s8[4718592]{0:T(1024)(128)(4,1)} %bitcast.137), calls=%async_computation.2 | async-start | bytes 1048576
  141.2 6.5 %copy-start.1 = (f32[1,2,3,96,1,2048]{5,3,2,1,0,4:T(8,128)S(1)}, f32[1,2,3,96,1,2048]{5,3,2,1,0,4:T(8,128)}, u32[]{:S(2)}) copy-start(f32[1,2,3,96,1,2048]{5,3,2,1,0,4:T(8,128)} %copy.79) | copy-start | bytes 14155780
  141.2 6.5 %copy-start.6 = (f32[3,96,2048]{2,1,0:T(8,128)S(1)}, f32[3,96,2048]{2,1,0:T(8,128)}, u32[]{:S(2)}) copy-start(f32[3,96,2048]{2,1,0:T(8,128)} %get-tuple-element.13) | copy-start | bytes 7077892
  141.2 7.1 %copy-start.7 = (f32[3,96,2048]{2,1,0:T(8,128)S(1)}, f32[3,96,2048]{2,1,0:T(8,128)}, u32[]{:S(2)}) copy-start(f32[3,96,2048]{2,1,0:T(8,128)} %get-tuple-element.14) | copy-start | bytes 7077892
  153.0 162.9 %collective-permute-start.2 = (f32[2,3,96,1,2048]{4,3,2,1,0:T(1,128)}, f32[2,3,96,1,2048]{4,3,2,1,0:T(1,128)S(1)}, u32[]{:S(2)}, u32[]{:S(2)}) collective-permute-start(f32[2,3,96,1,2048]{4,3,2,1,0:T(1,128)} %collective-permute-done), channel_id=1, source_target_pairs={{0,1},{1,2},{2,3},{3,0},{4,5},{5,6},{6,7},{7,4},{8,9},{9,10},{10,1... | collective-permute-start | bytes 14155784 | tf_op jit(solution)/shard_map/ppermute | solution.py:19
  412.7 3.4 copy-start.16
  412.7 4.6 copy-start.15
Sparse Core Ops, SparseCore 0:
  416.2 62.2 all-reduce.2
